TPU v7x, 512 devices: a whole 4x4x16 slice. The times are simulated.
512 devices in a mesh: row: 16 (over y, z_hi, core), col: 32 (over x, z_lo).
Axes of the slice: x: 4, y: 4, z: 16 (z_hi: 2, z_lo: 8; z = z_hi * 8 + z_lo), core: 2. Of those that a mesh axis runs over, the one named last changes fastest.
Arguments:
- latent: bfloat16 [16, 64, 128, 320], P(None, 'row', 'col'), may hold values from -6 to 6
- conv_weight: bfloat16 [2, 3, 3, 320, 320], replicated, may hold values from -0.109375 to 0.109375
- conv_gain: float32 [2, 320], replicated, may hold values from 0.25 to 1.75
- qkv_weight: bfloat16 [3, 2048, 320], P(None, 'col'), may hold values from -0.3125 to 0.3125
- qk_gain: bfloat16 [2, 2048], P(None, 'col'), may hold values from 0.6 to 9, as said below
- out_weight: bfloat16 [2048, 320], P('col'), may hold values from -0.5 to 0.5
Outputs:
- features: bfloat16 [16, 64, 128, 320], P(None, 'row', 'col')
- mixed: bfloat16 [16, 32, 64, 320], P('row', None, 'col')
Inputs may be any that keep to these rules, and one draw needn't show every extreme that they name: `qk_gain`: positive gains.
All inputs are finite; a program needn't handle non-finite values.
Results may differ from a plain program's by a relative error of at most 0.035.
Values may be sent and summed in bfloat16 or wider, within the bound.
No kernel may reach another device: no remote copies, remote signals or barrier semaphores. Data moves between devices by JAX's collectives and lax.ppermute only.
A program may use at most 64 MiB of HBM per device.

v0:
```python
import math
import jax
import jax.numpy as jnp
from jax import lax
from jax.sharding import PartitionSpec as P


def with_halo(array, sides, width):
    for axis, dim in sides:
        size, length = (lax.axis_size(axis), array.shape[dim])
        up = [(i, (i + 1) % size) for i in range(size)]
        down = [(j, i) for i, j in up]
        last = lax.slice_in_dim(array, length - width, length, axis=dim)
        leading = lax.slice_in_dim(array, 0, width, axis=dim)
        before = lax.ppermute(last, axis, up)
        after = lax.ppermute(leading, axis, down)
        array = jnp.concatenate([before, array, after], axis=dim)
    return array


def from_partner(array, axis, bit):
    return lax.ppermute(array, axis, [(i, i ^ 1 << bit) for i in range(lax.axis_size(axis))])


def rms_silu(hidden, gain_row):
    factor = lax.rsqrt(jnp.mean(hidden * hidden, axis=-1, keepdims=True) + 1e-06)
    return jax.nn.silu(hidden * factor * gain_row).astype(jnp.bfloat16)


def conv_taps(padded, kernels, out_rows, out_cols):
    image_count = padded.shape[0]
    channels = padded.shape[-1]
    total = jnp.zeros((image_count * out_rows * out_cols, kernels.shape[-1]), jnp.float32)
    for row_tap in range(3):
        for col_tap in range(3):
            window = padded[:, row_tap : row_tap + out_rows, col_tap : col_tap + out_cols]
            total = total + jnp.dot(
                window.reshape(image_count * out_rows * out_cols, channels),
                kernels[row_tap, col_tap],
                preferred_element_type=jnp.float32,
            )
    return total.reshape(image_count, out_rows, out_cols, kernels.shape[-1])


def head_norm(projected, gain_row):
    factor = lax.rsqrt(jnp.mean(projected * projected, axis=-1, keepdims=True) + 1e-06)
    return (projected * factor * gain_row.astype(jnp.float32)).astype(jnp.bfloat16)


def project(source, matrix):
    return lax.dot_general(
        source, matrix, (((1,), (1,)), ((), ())), preferred_element_type=jnp.float32
    )


def shards(latent, conv_weight, conv_gain, qkv_weight, qk_gain, out_weight):
    image_count, rows_tile, cols_tile, channels = latent.shape
    layer_count = conv_weight.shape[0]
    col_count = lax.axis_size("col")
    half_bit = lax.axis_index("col") % 2
    hidden = latent
    for layer_index in range(layer_count):
        activation = rms_silu(hidden.astype(jnp.float32), conv_gain[layer_index])
        padded = with_halo(activation, (("row", 1), ("col", 2)), 1)
        conv_sum = conv_taps(padded, conv_weight[layer_index], rows_tile, cols_tile)
        hidden = (hidden.astype(jnp.float32) + conv_sum).astype(jnp.bfloat16)
    tok_rows = rows_tile // 2
    tok_cols = cols_tile // 2
    pooled = (
        hidden.astype(jnp.float32)
        .reshape(image_count, tok_rows, 2, tok_cols, 2, channels)
        .mean(axis=(2, 4))
        .astype(jnp.bfloat16)
    )
    own_strip = lax.all_to_all(pooled, "row", split_axis=0, concat_axis=1, tiled=True)[0]
    image_tok = lax.all_gather(own_strip, "col", axis=1, tiled=True)
    partner_parts = from_partner((qkv_weight, qk_gain, out_weight), "col", 0)

    def join_halves(own_part, far_part, dim):
        lower_part = jnp.where(half_bit == 0, own_part, far_part)
        upper_part = jnp.where(half_bit == 0, far_part, own_part)
        return jnp.concatenate((lower_part, upper_part), dim)

    head_weight = join_halves(qkv_weight, partner_parts[0], 1)
    head_gain = join_halves(qk_gain, partner_parts[1], 1)
    head_out = join_halves(out_weight, partner_parts[2], 0)
    head_dim = head_weight.shape[1]
    scale = head_dim ** (-0.5)
    all_rows = image_tok.shape[0]
    all_tokens = image_tok.reshape(-1, channels)
    split_view = image_tok.reshape(all_rows, col_count, 2, tok_cols // 2, channels)
    own_tokens = lax.dynamic_index_in_dim(split_view, half_bit, 2, keepdims=False).reshape(
        -1, channels
    )
    own_count = own_tokens.shape[0]
    query_norm = head_norm(project(own_tokens, head_weight[0]), head_gain[0])
    key_norm = head_norm(project(all_tokens, head_weight[1]), head_gain[1])
    value_rows = project(all_tokens, head_weight[2]).astype(jnp.bfloat16)
    block_rows = math.gcd(own_count, 512)

    def one_block(query_block):
        scores = project(query_block, key_norm) * scale
        shifted = jnp.exp(scores - jnp.max(scores, axis=1, keepdims=True))
        return jnp.dot(
            shifted.astype(jnp.bfloat16), value_rows, preferred_element_type=jnp.float32
        ) / jnp.sum(shifted, axis=1, keepdims=True)

    attended = lax.map(one_block, query_norm.reshape(own_count // block_rows, block_rows, head_dim))
    attended = attended.reshape(own_count, head_dim).astype(jnp.bfloat16)
    head_terms = jnp.dot(attended, head_out, preferred_element_type=jnp.float32)
    head_terms = head_terms.reshape(all_rows, col_count, tok_cols // 2, channels)
    returned = lax.all_to_all(
        head_terms.astype(jnp.bfloat16), "col", split_axis=1, concat_axis=1, tiled=True
    ).astype(head_terms.dtype)
    summed = returned.reshape(all_rows, col_count // 2, 2, tok_cols // 2, channels).sum(axis=1)
    summed = summed.reshape(all_rows, tok_cols, channels)
    mixed = (own_strip.astype(jnp.float32) + summed).astype(jnp.bfloat16)
    return (hidden, mixed[None])


def solution(mesh):
    placed = (
        P(None, "row", "col", None),
        P(),
        P(),
        P(None, "col", None),
        P(None, "col"),
        P("col", None),
    )
    return jax.shard_map(
        shards,
        mesh=mesh,
        in_specs=placed,
        out_specs=(P(None, "row", "col", None), P("row", None, "col", None)),
        check_vma=False,
    )
```

profile of v0, /device:TPU:8, one launch (start us, length us, event | category | flops | bytes accessed | tf_op | source)
XLA Modules:
  0.0 428.7 jit_solution(16978137172392012358)
XLA Ops:
  7.2 0.8 slice_reduce_fusion
  8.0 1.1 fusion.23
  9.1 1.2 fusion.28
  10.4 1.9 collective-permute-start
  12.4 15.0 %collective-permute-start.1 = (bf16[16,1,4,320]{3,2,1,0:T(4,128)(2,1)S(1)}, bf16[16,1,4,320]{3,2,1,0:T(4,128)(2,1)S(1)}, u32[]{:S(2)}, u32[]{:S(2)}) collective-permute-start(bf16[16,1,4,320]{3,2,1,0:T(4,128)(2,1)S(1)} %get-tuple-element.121), channel_id=1, source_target_pairs={{32,0},{64,32},{96,64},{128,96},{160,128},{192,160},{224,192},{256... | collective-permute-start | bytes 122888 | tf_op jit(solution)/shard_map/ppermute | solution.py:16
  27.4 4.1 slice_bitcast_fusion
  31.5 0.8 reshape.165
  32.5 0.9 fusion.66
  33.5 2.9 collective-permute-start.2
  36.4 12.6 %collective-permute-start.3 = (bf16[16,6,1,320]{3,2,1,0:T(2,128)(2,1)}, bf16[16,6,1,320]{3,2,1,0:T(2,128)(2,1)S(1)}, u32[]{:S(2)}, u32[]{:S(2)}) collective-permute-start(bf16[16,6,1,320]{3,2,1,0:T(2,128)(2,1)} %get-tuple-element.113), channel_id=1, source_target_pairs={{1,0},{2,1},{3,2},{4,3},{5,4},{6,5},{7,6},{8,7},{9,8},{10,9},{11,1... | collective-permute-start | bytes 184328 | tf_op jit(solution)/shard_map/ppermute | solution.py:16
  49.3 1.2 fusion.40
  50.5 0.8 reshape.168
  51.3 0.6 collective-permute-done.3
  51.9 0.6 maximum_maximum_fusion
  52.5 1.1 fusion.63
  53.6 1.7 reshape.161
  55.3 0.8 reshape.163
  56.1 0.8 reshape.164
  57.1 1.4 fusion.39
  58.5 1.3 convolution_add_fusion.13
  59.9 1.3 convolution_add_fusion.12
  63.8 8.6 %collective-permute-start.4 = (bf16[16,1,4,320]{3,2,1,0:T(4,128)(2,1)S(1)}, bf16[16,1,4,320]{3,2,1,0:T(4,128)(2,1)S(1)}, u32[]{:S(2)}, u32[]{:S(2)}) collective-permute-start(bf16[16,1,4,320]{3,2,1,0:T(4,128)(2,1)S(1)} %get-tuple-element.116), channel_id=1, source_target_pairs={{0,32},{32,64},{64,96},{96,128},{128,160},{160,192},{192,224},{224... | collective-permute-start | bytes 122888 | tf_op jit(solution)/shard_map/ppermute | solution.py:15
  72.4 6.5 %collective-permute-start.5 = (bf16[16,1,4,320]{3,2,1,0:T(4,128)(2,1)S(1)}, bf16[16,1,4,320]{3,2,1,0:T(4,128)(2,1)S(1)}, u32[]{:S(2)}, u32[]{:S(2)}) collective-permute-start(bf16[16,1,4,320]{3,2,1,0:T(4,128)(2,1)S(1)} %get-tuple-element.117), channel_id=1, source_target_pairs={{32,0},{64,32},{96,64},{128,96},{160,128},{192,160},{224,192},{256... | collective-permute-start | bytes 122888 | tf_op jit(solution)/shard_map/ppermute | solution.py:16
  79.0 0.8 reshape.175
  79.7 1.0 collective-permute-done.5
  81.2 0.9 fusion.65
  82.2 1.9 collective-permute-start.6
  84.1 13.2 %collective-permute-start.7 = (bf16[16,6,1,320]{3,2,1,0:T(2,128)(2,1)}, bf16[16,6,1,320]{3,2,1,0:T(2,128)(2,1)}, u32[]{:S(2)}, u32[]{:S(2)}) collective-permute-start(bf16[16,6,1,320]{3,2,1,0:T(2,128)(2,1)} %get-tuple-element.109), channel_id=1, source_target_pairs={{1,0},{2,1},{3,2},{4,3},{5,4},{6,5},{7,6},{8,7},{9,8},{10,9},{11,1... | collective-permute-start | bytes 184328 | tf_op jit(solution)/shard_map/ppermute | solution.py:16
  97.6 0.8 reshape.178
  98.5 0.7 copy-done.17
  99.1 0.9 collective-permute-done.7
  100.0 1.7 maximum_maximum_fusion.1
  101.8 0.9 fusion.61
  102.7 1.7 reshape.171
  104.3 1.0 fusion.62
  105.3 1.7 reshape.173
  107.1 1.7 reshape.174
  108.8 1.0 reshape.176
  109.8 0.8 reshape.177
  110.5 1.1 reshape.179
  112.2 1.3 convolution_add_fusion.5
  116.2 32.2 %all_to_all.14 = bf16[16,2,2,320]{3,1,2,0:T(2,128)(2,1)S(1)} all-to-all(bf16[16,2,2,320]{3,1,2,0:T(2,128)(2,1)S(1)} %copy.78), channel_id=1, replica_groups=mesh['row'=16,'col'=32] {'row'}, dimensions={0} | all-to-all | bytes 81920 | tf_op jit(solution)/shard_map/all_to_all | solution.py:75
  148.5 0.6 copy.82
  149.1 1.9 collective-permute-start.8
  151.1 3.9 collective-permute-start.9
  155.1 1.9 collective-permute-start.10
  157.2 4.3 collective-permute-done.10
  161.5 0.7 broadcast_select_fusion.3
  162.2 209.3 %all-gather.2.cloned.1.call-done = bf16[32,64,320]{2,0,1:T(8,128)(2,1)} async-done(((bf16[32,2,320]{2,0,1:T(8,128)(2,1)}), bf16[32,64,320]{2,0,1:T(8,128)(2,1)}) %all-gather.2.cloned.1.call-update) | async-done | bytes 1310736 | tf_op jit(solution)/shard_map/all_gather | solution.py:76
  371.4 1.9 copy.84
  373.4 0.6 multiply_reduce_fusion.1
  374.0 0.6 convolution_convert_fusion
  375.8 0.5 multiply_reduce_fusion.2
  376.6 5.1 %while.10 = (s32[]{:T(128)}, bf16[2,512,128]{2,1,0:T(8,128)(2,1)S(1)}, bf16[2,512,128]{2,1,0:T(8,128)(2,1)S(1)}, bf16[2048,128]{1,0:T(8,128)(2,1)S(1)}, bf16[2048,128]{1,0:T(8,128)(2,1)S(1)}, /*index=5*/s32[]{:T(128)}) while((s32[]{:T(128)}, bf16[2,512,128]{2,1,0:T(8,128)(2,1)S(1)}, bf16[2,512,128]{2,1,0:T(8,128)(2,1)S(1)}, ...), condition=%wide.region_8.9_spmd, body=%wide.region_5.8_spmd.sunk | while | flops 545324032 | bytes 14035021 | solution.py:108
  376.6 0.8 multiply_reduce_fusion.4
  377.4 0.8 fusion.101
  378.2 0.9 fusion.102
  379.1 0.8 multiply_reduce_fusion.4
  379.9 0.8 fusion.101
  380.7 0.9 fusion.102
  382.1 1.2 copy.89
  383.3 11.5 %all-to-all-start.1 = ((bf16[32,32,1,320]{3,0,2,1:T(8,128)(2,1)}), bf16[32,32,1,320]{3,0,2,1:T(8,128)(2,1)S(1)}, u32[]{:S(2)}, u32[]{:S(2)}) async-start(bf16[32,32,1,320]{3,0,2,1:T(8,128)(2,1)} %copy.89), calls=%async_computation.1 | async-start | bytes 1572864 | tf_op jit(solution)/shard_map/all_to_all | solution.py:112
  394.8 26.2 %all-to-all-done.1 = bf16[32,32,1,320]{3,0,2,1:T(8,128)(2,1)S(1)} async-done(((bf16[32,32,1,320]{3,0,2,1:T(8,128)(2,1)}), bf16[32,32,1,320]{3,0,2,1:T(8,128)(2,1)S(1)}, u32[]{:S(2)}, u32[]{:S(2)}) %all-to-all-start.1) | async-done | bytes 655392 | tf_op jit(solution)/shard_map/all_to_all | solution.py:112
  421.2 0.7 copy.91
  (106 shorter events, 9.8 us)
Async XLA Ops:
  7.2 364.3 %all-gather.2.cloned.1.call-start = ((), (), s32[]{:S(2)}) async-start(), calls=%async_computation.2 | async-start | bytes 1622016 | tf_op jit(solution)/shard_map/all_gather | solution.py:76
  10.4 21.9 %collective-permute-start = (bf16[16,1,4,320]{3,2,1,0:T(4,128)(2,1)S(1)}, bf16[16,1,4,320]{3,2,1,0:T(4,128)(2,1)S(1)}, u32[]{:S(2)}, u32[]{:S(2)}) collective-permute-start(bf16[16,1,4,320]{3,2,1,0:T(4,128)(2,1)S(1)} %get-tuple-element.120), channel_id=1, source_target_pairs={{0,32},{32,64},{64,96},{96,128},{128,160},{160,192},{192,224},{224... | collective-permute-start | bytes 122888 | tf_op jit(solution)/shard_map/ppermute | solution.py:15
  12.4 20.0 %collective-permute-start.1 = (bf16[16,1,4,320]{3,2,1,0:T(4,128)(2,1)S(1)}, bf16[16,1,4,320]{3,2,1,0:T(4,128)(2,1)S(1)}, u32[]{:S(2)}, u32[]{:S(2)}) collective-permute-start(bf16[16,1,4,320]{3,2,1,0:T(4,128)(2,1)S(1)} %get-tuple-element.121), channel_id=1, source_target_pairs={{32,0},{64,32},{96,64},{128,96},{160,128},{192,160},{224,192},{256... | collective-permute-start | bytes 122888 | tf_op jit(solution)/shard_map/ppermute | solution.py:16
  33.5 17.8 %collective-permute-start.2 = (bf16[16,6,1,320]{3,2,1,0:T(2,128)(2,1)}, bf16[16,6,1,320]{3,2,1,0:T(2,128)(2,1)S(1)}, u32[]{:S(2)}, u32[]{:S(2)}) collective-permute-start(bf16[16,6,1,320]{3,2,1,0:T(2,128)(2,1)} %get-tuple-element.112), channel_id=1, source_target_pairs={{0,1},{1,2},{2,3},{3,4},{4,5},{5,6},{6,7},{7,8},{8,9},{9,10},{10,1... | collective-permute-start | bytes 184328 | tf_op jit(solution)/shard_map/ppermute | solution.py:15
  36.4 15.5 %collective-permute-start.3 = (bf16[16,6,1,320]{3,2,1,0:T(2,128)(2,1)}, bf16[16,6,1,320]{3,2,1,0:T(2,128)(2,1)S(1)}, u32[]{:S(2)}, u32[]{:S(2)}) collective-permute-start(bf16[16,6,1,320]{3,2,1,0:T(2,128)(2,1)} %get-tuple-element.113), channel_id=1, source_target_pairs={{1,0},{2,1},{3,2},{4,3},{5,4},{6,5},{7,6},{8,7},{9,8},{10,9},{11,1... | collective-permute-start | bytes 184328 | tf_op jit(solution)/shard_map/ppermute | solution.py:16
  57.0 4.5 %copy-start.5 = (bf16[256,320]{1,0:T(8,128)(2,1)S(1)}, bf16[256,320]{1,0:T(8,128)(2,1)}, u32[]{:S(2)}) copy-start(bf16[256,320]{1,0:T(8,128)(2,1)} %reshape.165) | copy-start | bytes 491524
  57.1 4.1 copy-start
  57.1 4.1 copy-start.11
  61.2 1.3 copy-start.7
  62.2 0.9 copy-start.2
  63.8 16.0 %collective-permute-start.4 = (bf16[16,1,4,320]{3,2,1,0:T(4,128)(2,1)S(1)}, bf16[16,1,4,320]{3,2,1,0:T(4,128)(2,1)S(1)}, u32[]{:S(2)}, u32[]{:S(2)}) collective-permute-start(bf16[16,1,4,320]{3,2,1,0:T(4,128)(2,1)S(1)} %get-tuple-element.116), channel_id=1, source_target_pairs={{0,32},{32,64},{64,96},{96,128},{128,160},{160,192},{192,224},{224... | collective-permute-start | bytes 122888 | tf_op jit(solution)/shard_map/ppermute | solution.py:15
  72.4 8.3 %collective-permute-start.5 = (bf16[16,1,4,320]{3,2,1,0:T(4,128)(2,1)S(1)}, bf16[16,1,4,320]{3,2,1,0:T(4,128)(2,1)S(1)}, u32[]{:S(2)}, u32[]{:S(2)}) collective-permute-start(bf16[16,1,4,320]{3,2,1,0:T(4,128)(2,1)S(1)} %get-tuple-element.117), channel_id=1, source_target_pairs={{32,0},{64,32},{96,64},{128,96},{160,128},{192,160},{224,192},{256... | collective-permute-start | bytes 122888 | tf_op jit(solution)/shard_map/ppermute | solution.py:16
  79.7 17.5 %copy-start.12 = (bf16[16,1,4,320]{3,2,1,0:T(4,128)(2,1)}, bf16[16,1,4,320]{3,2,1,0:T(4,128)(2,1)S(1)}, u32[]{:S(2)}) copy-start(bf16[16,1,4,320]{3,2,1,0:T(4,128)(2,1)S(1)} %collective-permute-done.4) | copy-start | bytes 122884
  80.7 16.6 %copy-start.13 = (bf16[16,1,4,320]{3,2,1,0:T(4,128)(2,1)}, bf16[16,1,4,320]{3,2,1,0:T(4,128)(2,1)S(1)}, u32[]{:S(2)}) copy-start(bf16[16,1,4,320]{3,2,1,0:T(4,128)(2,1)S(1)} %collective-permute-done.5) | copy-start | bytes 122884
  82.2 16.3 %collective-permute-start.6 = (bf16[16,6,1,320]{3,2,1,0:T(2,128)(2,1)}, bf16[16,6,1,320]{3,2,1,0:T(2,128)(2,1)S(1)}, u32[]{:S(2)}, u32[]{:S(2)}) collective-permute-start(bf16[16,6,1,320]{3,2,1,0:T(2,128)(2,1)} %get-tuple-element.108), channel_id=1, source_target_pairs={{0,1},{1,2},{2,3},{3,4},{4,5},{5,6},{6,7},{7,8},{8,9},{9,10},{10,1... | collective-permute-start | bytes 184328 | tf_op jit(solution)/shard_map/ppermute | solution.py:15
  84.1 16.0 %collective-permute-start.7 = (bf16[16,6,1,320]{3,2,1,0:T(2,128)(2,1)}, bf16[16,6,1,320]{3,2,1,0:T(2,128)(2,1)}, u32[]{:S(2)}, u32[]{:S(2)}) collective-permute-start(bf16[16,6,1,320]{3,2,1,0:T(2,128)(2,1)} %get-tuple-element.109), channel_id=1, source_target_pairs={{1,0},{2,1},{3,2},{4,3},{5,4},{6,5},{7,6},{8,7},{9,8},{10,9},{11,1... | collective-permute-start | bytes 184328 | tf_op jit(solution)/shard_map/ppermute | solution.py:16
  98.5 0.7 copy-start.17
  105.3 6.6 %copy-start.8 = (bf16[256,320]{1,0:T(8,128)(2,1)S(1)}, bf16[256,320]{1,0:T(8,128)(2,1)}, u32[]{:S(2)}) copy-start(bf16[256,320]{1,0:T(8,128)(2,1)} %reshape.171) | copy-start | bytes 491524
  110.5 3.3 copy-start.4
  111.6 1.9 copy-start.10
  112.2 2.2 copy-start.9
  113.5 1.2 copy-start.6
  115.1 34.0 %copy-start.18 = (bf16[3,64,320]{2,1,0:T(8,128)(2,1)S(1)}, bf16[3,64,320]{2,1,0:T(8,128)(2,1)}, u32[]{:S(2)}) copy-start(bf16[3,64,320]{2,1,0:T(8,128)(2,1)} %param.11) | copy-start | bytes 368644
  115.1 36.0 %copy-start.20 = (bf16[2,64]{1,0:T(2,128)(2,1)S(1)}, bf16[2,64]{1,0:T(2,128)(2,1)}, u32[]{:S(2)}) copy-start(bf16[2,64]{1,0:T(2,128)(2,1)} %param.12) | copy-start | bytes 772
  115.1 39.9 %copy-start.19 = (bf16[64,320]{1,0:T(8,128)(2,1)S(1)}, bf16[64,320]{1,0:T(8,128)(2,1)}, u32[]{:S(2)}) copy-start(bf16[64,320]{1,0:T(8,128)(2,1)} %param.13) | copy-start | bytes 122884
  115.5 257.9 %copy-start.3 = (bf16[16,4,4,320]{3,2,1,0:T(4,128)(2,1)}, bf16[16,4,4,320]{3,2,1,0:T(4,128)(2,1)S(1)}, u32[]{:S(2)}) copy-start(bf16[16,4,4,320]{3,2,1,0:T(4,128)(2,1)S(1)} %fusion.36) | copy-start | bytes 491524
  149.1 13.0 %collective-permute-start.8 = (bf16[3,64,320]{2,1,0:T(8,128)(2,1)S(1)}, bf16[3,64,320]{2,1,0:T(8,128)(2,1)S(1)}, u32[]{:S(2)}, u32[]{:S(2)}) collective-permute-start(bf16[3,64,320]{2,1,0:T(8,128)(2,1)S(1)} %copy-done.18), channel_id=1, source_target_pairs={{0,1},{1,0},{2,3},{3,2},{4,5},{5,4},{6,7},{7,6},{8,9},{9,8},{10,11... | collective-permute-start | bytes 368648 | tf_op jit(solution)/shard_map/ppermute | solution.py:22
  151.1 6.0 %collective-permute-start.9 = (bf16[2,64]{1,0:T(2,128)(2,1)S(1)}, bf16[2,64]{1,0:T(2,128)(2,1)S(1)}, u32[]{:S(2)}, u32[]{:S(2)}) collective-permute-start(bf16[2,64]{1,0:T(2,128)(2,1)S(1)} %copy-done.20), channel_id=1, source_target_pairs={{0,1},{1,0},{2,3},{3,2},{4,5},{5,4},{6,7},{7,6},{8,9},{9,8},{10,11... | collective-permute-start | bytes 776 | tf_op jit(solution)/shard_map/ppermute | solution.py:22
  155.1 6.3 %collective-permute-start.10 = (bf16[64,320]{0,1:T(8,128)(2,1)S(1)}, bf16[64,320]{0,1:T(8,128)(2,1)S(1)}, u32[]{:S(2)}, u32[]{:S(2)}) collective-permute-start(bf16[64,320]{0,1:T(8,128)(2,1)S(1)} %copy.87), channel_id=1, source_target_pairs={{0,1},{1,0},{2,3},{3,2},{4,5},{5,4},{6,7},{7,6},{8,9},{9,8},{10,11... | collective-permute-start | bytes 122888 | tf_op jit(solution)/shard_map/ppermute | solution.py:22
  374.0 1.4 copy-start.1
  375.5 1.0 copy-start.16
  376.5 5.1 %copy-start.14 = (bf16[64,320]{0,1:T(8,128)(2,1)S(1)}, bf16[64,320]{0,1:T(8,128)(2,1)}, u32[]{:S(2)}) copy-start(bf16[64,320]{0,1:T(8,128)(2,1)} %get-tuple-element.122) | copy-start | bytes 122884
  376.5 5.1 %copy-start.15 = (bf16[64,320]{0,1:T(8,128)(2,1)S(1)}, bf16[64,320]{0,1:T(8,128)(2,1)}, u32[]{:S(2)}) copy-start(bf16[64,320]{0,1:T(8,128)(2,1)} %get-tuple-element.123) | copy-start | bytes 122884
  383.3 37.8 %all-to-all-start.1 = ((bf16[32,32,1,320]{3,0,2,1:T(8,128)(2,1)}), bf16[32,32,1,320]{3,0,2,1:T(8,128)(2,1)S(1)}, u32[]{:S(2)}, u32[]{:S(2)}) async-start(bf16[32,32,1,320]{3,0,2,1:T(8,128)(2,1)} %copy.89), calls=%async_computation.1 | async-start | bytes 1572864 | tf_op jit(solution)/shard_map/all_to_all | solution.py:112
Sparse Core Ops, SparseCore 0:
  149.2 222.1 all-gather.1
where the time goes:
time: 430 us; the launch traced here: 429 us
  waiting for transfers between devices  242 us (56%)
  starting transfers between devices  82 us (19%)
  blocking collectives  32.2 us (7%)
  local copies, waits for them, and re-layouts  31.6 us (7%)
  matrix products  16 us (4%)
  between operations  14.9 us (3%)
  other arithmetic  9.61 us (2%)
    all_gather x1, waiting for transfers between devices, shards(): image_tok = lax.all_gather(own_strip, 'col', axis=1, tiled=True)  209 us
    ppermute x4, starting transfers between devices, with_halo(): after = lax.ppermute(leading, axis, down)  47.3 us
    all_to_all x1, blocking collectives, shards(): lax.all_to_all(pooled, 'row', split_axis=0, concat_axis=1, tiled=True)[0]  32.2 us
    all_to_all x1, waiting for transfers between devices, shards(): lax.all_to_all(head_terms.astype(jnp.bfloat16), 'col', split_axis=1, conc...  26.2 us
    ppermute x4, starting transfers between devices, with_halo(): before = lax.ppermute(last, axis, up)  15.4 us
    reshape x18, local copies, waits for them, and re-layouts, conv_taps(): window.reshape(image_count * out_rows * out_cols, channels)  14.7 us
    all_to_all x1, starting transfers between devices, shards(): lax.all_to_all(head_terms.astype(jnp.bfloat16), 'col', split_axis=1, conc...  11.5 us
    dot_general x18, matrix products, conv_taps(): jnp.dot(window.reshape(image_count * out_rows * out_cols, channels), kern...  10.4 us
  transfers between devices with their start and end apart: 13, of which 7 were waited for; matrix products, arithmetic and copies ran while one was open for 2% of the time, Pallas kernels for 0%

commit v1 on v0

--- a/solution.py
+++ b/solution.py
@@ -73,7 +73,8 @@
         .astype(jnp.bfloat16)
     )
     own_strip = lax.all_to_all(pooled, "row", split_axis=0, concat_axis=1, tiled=True)[0]
-    image_tok = lax.all_gather(own_strip, "col", axis=1, tiled=True)
+    outgoing = jnp.stack([own_strip] * lax.axis_size("col"))
+    image_tok = jnp.concatenate(lax.all_to_all(outgoing, "col", 0, 0), axis=1)
     partner_parts = from_partner((qkv_weight, qk_gain, out_weight), "col", 0)
 
     def join_halves(own_part, far_part, dim):

time: 430 us -> 301 us (0.70)
  the two profiles are of different devices: /device:TPU:8 before, /device:TPU:1 now
where the time goes in v1:
time: 301 us; the launch traced here: 300 us
  waiting for transfers between devices  122 us (41%)
  starting transfers between devices  83.5 us (28%)
  local copies, waits for them, and re-layouts  41.6 us (14%)
  blocking collectives  24.1 us (8%)
  matrix products  17.7 us (6%)
  other arithmetic  9.61 us (3%)
    all_to_all x1, waiting for transfers between devices, shards(): lax.all_to_all(head_terms.astype(jnp.bfloat16), 'col', split_axis=1, conc...  39.8 us
    all_to_all x1, waiting for transfers between devices, shards(): image_tok = jnp.concatenate(lax.all_to_all(outgoing, 'col', 0, 0), axis=1)  36.7 us
    ppermute x4, starting transfers between devices, with_halo(): after = lax.ppermute(leading, axis, down)  28.8 us
    ppermute x4, starting transfers between devices, with_halo(): before = lax.ppermute(last, axis, up)  25.3 us
    ppermute x3, waiting for transfers between devices, from_partner(): lax.ppermute(array, axis, [(i, i ^ 1 << bit) for i in range(lax.axis_size...  25.2 us
    all_to_all x1, blocking collectives, shards(): lax.all_to_all(pooled, 'row', split_axis=0, concat_axis=1, tiled=True)[0]  24.1 us
    ppermute x4, waiting for transfers between devices, with_halo(): after = lax.ppermute(leading, axis, down)  20.5 us
    reshape x18, local copies, waits for them, and re-layouts, conv_taps(): window.reshape(image_count * out_rows * out_cols, channels)  16 us
  transfers between devices with their start and end apart: 13, of which 8 were waited for; matrix products, arithmetic and copies ran while one was open for 4% of the time, Pallas kernels for 0%

profile of v1, /device:TPU:1, one launch (start us, length us, event | category | flops | bytes accessed | tf_op | source)
XLA Modules:
  0.0 300.3 jit_solution(9218703271240708276)
XLA Ops:
  0.6 0.8 slice_reduce_fusion
  1.4 1.1 fusion.23
  2.6 1.2 fusion.28
  3.8 16.8 %collective-permute-start = (bf16[16,1,4,320]{3,2,1,0:T(4,128)(2,1)S(1)}, bf16[16,1,4,320]{3,2,1,0:T(4,128)(2,1)S(1)}, u32[]{:S(2)}, u32[]{:S(2)}) collective-permute-start(bf16[16,1,4,320]{3,2,1,0:T(4,128)(2,1)S(1)} %get-tuple-element.126), channel_id=1, source_target_pairs={{0,32},{32,64},{64,96},{96,128},{128,160},{160,192},{192,224},{224... | collective-permute-start | bytes 122888 | tf_op jit(solution)/shard_map/ppermute | solution.py:15
  20.7 1.9 collective-permute-start.1
  22.6 4.1 %slice_bitcast_fusion = (bf16[3,3,320,320]{3,2,1,0:T(8,128)(2,1)S(1)}, bf16[3,3,320,320]{3,2,1,0:T(8,128)(2,1)}) fusion(bf16[2,3,3,320,320]{4,3,2,1,0:T(8,128)(2,1)} %param.9), kind=kLoop, calls=%fused_computation.16 | loop fusion | bytes 7372800 | tf_op jit(solution)/shard_map/squeeze | solution.py:65
  26.7 0.8 reshape.167
  27.5 8.9 %collective-permute-done.1 = bf16[16,1,4,320]{3,2,1,0:T(4,128)(2,1)S(1)} collective-permute-done((bf16[16,1,4,320]{3,2,1,0:T(4,128)(2,1)S(1)}, bf16[16,1,4,320]{3,2,1,0:T(4,128)(2,1)S(1)}, u32[]{:S(2)}, u32[]{:S(2)}) %collective-permute-start.1) | collective-permute-done | bytes 40992 | tf_op jit(solution)/shard_map/ppermute | solution.py:16
  36.6 0.9 fusion.66
  37.5 1.9 collective-permute-start.2
  39.4 12.1 %collective-permute-start.3 = (bf16[16,6,1,320]{3,2,1,0:T(2,128)(2,1)}, bf16[16,6,1,320]{3,2,1,0:T(2,128)(2,1)S(1)}, u32[]{:S(2)}, u32[]{:S(2)}) collective-permute-start(bf16[16,6,1,320]{3,2,1,0:T(2,128)(2,1)} %get-tuple-element.119), channel_id=1, source_target_pairs={{1,0},{2,1},{3,2},{4,3},{5,4},{6,5},{7,6},{8,7},{9,8},{10,9},{11,1... | collective-permute-start | bytes 184328 | tf_op jit(solution)/shard_map/ppermute | solution.py:16
  51.8 1.2 fusion.40
  53.1 0.8 reshape.170
  54.5 1.1 fusion.63
  55.6 1.7 reshape.163
  57.3 0.8 reshape.165
  58.1 0.8 reshape.166
  59.2 1.4 fusion.39
  60.6 1.3 convolution_add_fusion.13
  61.9 1.3 convolution_add_fusion.12
  65.8 4.6 %collective-permute-start.4 = (bf16[16,1,4,320]{3,2,1,0:T(4,128)(2,1)S(1)}, bf16[16,1,4,320]{3,2,1,0:T(4,128)(2,1)S(1)}, u32[]{:S(2)}, u32[]{:S(2)}) collective-permute-start(bf16[16,1,4,320]{3,2,1,0:T(4,128)(2,1)S(1)} %get-tuple-element.122), channel_id=1, source_target_pairs={{0,32},{32,64},{64,96},{96,128},{128,160},{160,192},{192,224},{224... | collective-permute-start | bytes 122888 | tf_op jit(solution)/shard_map/ppermute | solution.py:15
  70.4 1.9 collective-permute-start.5
  72.3 0.8 reshape.177
  73.1 11.5 %collective-permute-done.5 = bf16[16,1,4,320]{3,2,1,0:T(4,128)(2,1)S(1)} collective-permute-done((bf16[16,1,4,320]{3,2,1,0:T(4,128)(2,1)S(1)}, bf16[16,1,4,320]{3,2,1,0:T(4,128)(2,1)S(1)}, u32[]{:S(2)}, u32[]{:S(2)}) %collective-permute-start.5) | collective-permute-done | bytes 40992 | tf_op jit(solution)/shard_map/ppermute | solution.py:16
  84.9 0.8 reshape.174
  85.9 0.9 fusion.65
  86.8 1.9 collective-permute-start.6
  88.7 12.9 %collective-permute-start.7 = (bf16[16,6,1,320]{3,2,1,0:T(2,128)(2,1)}, bf16[16,6,1,320]{3,2,1,0:T(2,128)(2,1)}, u32[]{:S(2)}, u32[]{:S(2)}) collective-permute-start(bf16[16,6,1,320]{3,2,1,0:T(2,128)(2,1)} %get-tuple-element.115), channel_id=1, source_target_pairs={{1,0},{2,1},{3,2},{4,3},{5,4},{6,5},{7,6},{8,7},{9,8},{10,9},{11,1... | collective-permute-start | bytes 184328 | tf_op jit(solution)/shard_map/ppermute | solution.py:16
  101.6 1.2 fusion.38
  102.9 0.8 reshape.180
  104.4 1.7 maximum_maximum_fusion.1
  106.1 0.9 fusion.61
  107.0 1.7 reshape.173
  108.7 1.0 fusion.62
  109.7 1.7 reshape.175
  111.4 1.7 reshape.176
  113.1 1.7 reshape.178
  114.8 0.8 reshape.179
  115.6 1.0 reshape.181
  117.3 1.3 convolution_add_fusion.5
  121.3 24.1 %all_to_all.22 = bf16[16,2,2,320]{3,1,2,0:T(2,128)(2,1)S(1)} all-to-all(bf16[16,2,2,320]{3,1,2,0:T(2,128)(2,1)S(1)} %copy.82), channel_id=1, replica_groups=mesh['row'=16,'col'=32] {'row'}, dimensions={0} | all-to-all | bytes 81920 | tf_op jit(solution)/shard_map/all_to_all | solution.py:75
  145.4 2.6 stack.3
  148.0 11.8 %all-to-all-start.1 = ((bf16[32,32,2,320]{3,2,1,0:T(2,128)(2,1)}), bf16[32,32,2,320]{3,2,1,0:T(2,128)(2,1)S(1)}, u32[]{:S(2)}, u32[]{:S(2)}) async-start(bf16[32,32,2,320]{3,2,1,0:T(2,128)(2,1)} %stack.3), calls=%async_computation.1 | async-start | bytes 3145728 | tf_op jit(solution)/shard_map/all_to_all | solution.py:77
  159.8 3.1 %collective-permute-start.8 = (bf16[3,64,320]{2,1,0:T(8,128)(2,1)S(1)}, bf16[3,64,320]{2,1,0:T(8,128)(2,1)S(1)}, u32[]{:S(2)}, u32[]{:S(2)}) collective-permute-start(bf16[3,64,320]{2,1,0:T(8,128)(2,1)S(1)} %copy-done.19), channel_id=1, source_target_pairs={{0,1},{1,0},{2,3},{3,2},{4,5},{5,4},{6,7},{7,6},{8,9},{9,8},{10,11... | collective-permute-start | bytes 368648 | tf_op jit(solution)/shard_map/ppermute | solution.py:22
  163.0 2.1 collective-permute-start.9
  165.3 3.4 %collective-permute-start.10 = (bf16[64,320]{0,1:T(8,128)(2,1)S(1)}, bf16[64,320]{0,1:T(8,128)(2,1)S(1)}, u32[]{:S(2)}, u32[]{:S(2)}) collective-permute-start(bf16[64,320]{0,1:T(8,128)(2,1)S(1)} %copy.90), channel_id=1, source_target_pairs={{0,1},{1,0},{2,3},{3,2},{4,5},{5,4},{6,7},{7,6},{8,9},{9,8},{10,11... | collective-permute-start | bytes 122888 | tf_op jit(solution)/shard_map/ppermute | solution.py:22
  168.7 23.6 %collective-permute-done.9 = bf16[2,64]{1,0:T(2,128)(2,1)S(1)} collective-permute-done((bf16[2,64]{1,0:T(2,128)(2,1)S(1)}, bf16[2,64]{1,0:T(2,128)(2,1)S(1)}, u32[]{:S(2)}, u32[]{:S(2)}) %collective-permute-start.9) | collective-permute-done | bytes 288 | tf_op jit(solution)/shard_map/ppermute | solution.py:22
  192.3 1.6 collective-permute-done.10
  194.7 36.7 %all-to-all-done.1 = bf16[32,32,2,320]{3,2,1,0:T(2,128)(2,1)S(1)} async-done(((bf16[32,32,2,320]{3,2,1,0:T(2,128)(2,1)}), bf16[32,32,2,320]{3,2,1,0:T(2,128)(2,1)S(1)}, u32[]{:S(2)}, u32[]{:S(2)}) %all-to-all-start.1) | async-done | bytes 1310752 | tf_op jit(solution)/shard_map/all_to_all | solution.py:77
  231.3 2.9 copy.87
  234.2 3.7 %reshape_reshape.4 = bf16[2048,320]{1,0:T(8,128)(2,1)S(1)} reshape(bf16[32,32,2,320]{3,2,1,0:T(2,128)(2,1)} %copy.87) | data formatting | bytes 2621440 | tf_op jit(solution)/shard_map/reshape;reshape | solution.py:91
  238.5 1.4 convolution_convert_fusion
  240.3 1.9 dynamic-slice_bitcast_fusion
  242.3 0.9 copy.86
  243.9 5.1 %while.10 = (s32[]{:T(128)}, bf16[2,512,128]{2,1,0:T(8,128)(2,1)S(1)}, bf16[2,512,128]{2,1,0:T(8,128)(2,1)S(1)}, bf16[2048,128]{1,0:T(8,128)(2,1)S(1)}, bf16[2048,128]{1,0:T(8,128)(2,1)S(1)}, /*index=5*/s32[]{:T(128)}) while((s32[]{:T(128)}, bf16[2,512,128]{2,1,0:T(8,128)(2,1)S(1)}, bf16[2,512,128]{2,1,0:T(8,128)(2,1)S(1)}, ...), condition=%wide.region_8.9_spmd, body=%wide.region_5.8_spmd.sunk | while | flops 545324032 | bytes 14035021 | solution.py:109
  243.9 0.8 multiply_reduce_fusion.4
  244.7 0.8 fusion.101
  245.5 0.9 fusion.102
  246.4 0.8 multiply_reduce_fusion.4
  247.2 0.8 fusion.101
  248.0 0.9 fusion.102
  249.4 1.2 copy.92
  250.6 9.0 %all-to-all-start.2 = ((bf16[32,32,1,320]{3,0,2,1:T(8,128)(2,1)}), bf16[32,32,1,320]{3,0,2,1:T(8,128)(2,1)S(1)}, u32[]{:S(2)}, u32[]{:S(2)}) async-start(bf16[32,32,1,320]{3,0,2,1:T(8,128)(2,1)} %copy.92), calls=%async_computation.2 | async-start | bytes 1572864 | tf_op jit(solution)/shard_map/all_to_all | solution.py:113
  259.6 39.8 %all-to-all-done.2 = bf16[32,32,1,320]{3,0,2,1:T(8,128)(2,1)S(1)} async-done(((bf16[32,32,1,320]{3,0,2,1:T(8,128)(2,1)}), bf16[32,32,1,320]{3,0,2,1:T(8,128)(2,1)S(1)}, u32[]{:S(2)}, u32[]{:S(2)}) %all-to-all-start.2) | async-done | bytes 655392 | tf_op jit(solution)/shard_map/all_to_all | solution.py:113
  (108 shorter events, 12.4 us)
Async XLA Ops:
  3.8 23.7 %collective-permute-start = (bf16[16,1,4,320]{3,2,1,0:T(4,128)(2,1)S(1)}, bf16[16,1,4,320]{3,2,1,0:T(4,128)(2,1)S(1)}, u32[]{:S(2)}, u32[]{:S(2)}) collective-permute-start(bf16[16,1,4,320]{3,2,1,0:T(4,128)(2,1)S(1)} %get-tuple-element.126), channel_id=1, source_target_pairs={{0,32},{32,64},{64,96},{96,128},{128,160},{160,192},{192,224},{224... | collective-permute-start | bytes 122888 | tf_op jit(solution)/shard_map/ppermute | solution.py:15
  20.7 15.7 %collective-permute-start.1 = (bf16[16,1,4,320]{3,2,1,0:T(4,128)(2,1)S(1)}, bf16[16,1,4,320]{3,2,1,0:T(4,128)(2,1)S(1)}, u32[]{:S(2)}, u32[]{:S(2)}) collective-permute-start(bf16[16,1,4,320]{3,2,1,0:T(4,128)(2,1)S(1)} %get-tuple-element.127), channel_id=1, source_target_pairs={{32,0},{64,32},{96,64},{128,96},{160,128},{192,160},{224,192},{256... | collective-permute-start | bytes 122888 | tf_op jit(solution)/shard_map/ppermute | solution.py:16
  37.5 16.3 %collective-permute-start.2 = (bf16[16,6,1,320]{3,2,1,0:T(2,128)(2,1)}, bf16[16,6,1,320]{3,2,1,0:T(2,128)(2,1)S(1)}, u32[]{:S(2)}, u32[]{:S(2)}) collective-permute-start(bf16[16,6,1,320]{3,2,1,0:T(2,128)(2,1)} %get-tuple-element.118), channel_id=1, source_target_pairs={{0,1},{1,2},{2,3},{3,4},{4,5},{5,6},{6,7},{7,8},{8,9},{9,10},{10,1... | collective-permute-start | bytes 184328 | tf_op jit(solution)/shard_map/ppermute | solution.py:15
  39.4 14.5 %collective-permute-start.3 = (bf16[16,6,1,320]{3,2,1,0:T(2,128)(2,1)}, bf16[16,6,1,320]{3,2,1,0:T(2,128)(2,1)S(1)}, u32[]{:S(2)}, u32[]{:S(2)}) collective-permute-start(bf16[16,6,1,320]{3,2,1,0:T(2,128)(2,1)} %get-tuple-element.119), channel_id=1, source_target_pairs={{1,0},{2,1},{3,2},{4,3},{5,4},{6,5},{7,6},{8,7},{9,8},{10,9},{11,1... | collective-permute-start | bytes 184328 | tf_op jit(solution)/shard_map/ppermute | solution.py:16
  59.0 4.5 %copy-start.4 = (bf16[256,320]{1,0:T(8,128)(2,1)S(1)}, bf16[256,320]{1,0:T(8,128)(2,1)}, u32[]{:S(2)}) copy-start(bf16[256,320]{1,0:T(8,128)(2,1)} %reshape.167) | copy-start | bytes 491524
  59.1 4.1 %copy-start = (bf16[3,3,320,320]{3,2,1,0:T(8,128)(2,1)S(1)}, bf16[3,3,320,320]{3,2,1,0:T(8,128)(2,1)}, u32[]{:S(2)}) copy-start(bf16[3,3,320,320]{3,2,1,0:T(8,128)(2,1)} %get-tuple-element.97) | copy-start | bytes 5529604
  59.1 4.1 %copy-start.11 = (bf16[256,320]{1,0:T(8,128)(2,1)S(1)}, bf16[256,320]{1,0:T(8,128)(2,1)}, u32[]{:S(2)}) copy-start(bf16[256,320]{1,0:T(8,128)(2,1)} %reshape.166) | copy-start | bytes 491524
  63.3 1.3 copy-start.6
  64.2 0.9 copy-start.1
  65.8 7.3 %collective-permute-start.4 = (bf16[16,1,4,320]{3,2,1,0:T(4,128)(2,1)S(1)}, bf16[16,1,4,320]{3,2,1,0:T(4,128)(2,1)S(1)}, u32[]{:S(2)}, u32[]{:S(2)}) collective-permute-start(bf16[16,1,4,320]{3,2,1,0:T(4,128)(2,1)S(1)} %get-tuple-element.122), channel_id=1, source_target_pairs={{0,32},{32,64},{64,96},{96,128},{128,160},{160,192},{192,224},{224... | collective-permute-start | bytes 122888 | tf_op jit(solution)/shard_map/ppermute | solution.py:15
  70.4 14.2 %collective-permute-start.5 = (bf16[16,1,4,320]{3,2,1,0:T(4,128)(2,1)S(1)}, bf16[16,1,4,320]{3,2,1,0:T(4,128)(2,1)S(1)}, u32[]{:S(2)}, u32[]{:S(2)}) collective-permute-start(bf16[16,1,4,320]{3,2,1,0:T(4,128)(2,1)S(1)} %get-tuple-element.123), channel_id=1, source_target_pairs={{32,0},{64,32},{96,64},{128,96},{160,128},{192,160},{224,192},{256... | collective-permute-start | bytes 122888 | tf_op jit(solution)/shard_map/ppermute | solution.py:16
  73.1 30.6 %copy-start.13 = (bf16[16,1,4,320]{3,2,1,0:T(4,128)(2,1)}, bf16[16,1,4,320]{3,2,1,0:T(4,128)(2,1)S(1)}, u32[]{:S(2)}) copy-start(bf16[16,1,4,320]{3,2,1,0:T(4,128)(2,1)S(1)} %collective-permute-done.4) | copy-start | bytes 122884
  84.6 19.1 %copy-start.14 = (bf16[16,1,4,320]{3,2,1,0:T(4,128)(2,1)}, bf16[16,1,4,320]{3,2,1,0:T(4,128)(2,1)S(1)}, u32[]{:S(2)}) copy-start(bf16[16,1,4,320]{3,2,1,0:T(4,128)(2,1)S(1)} %collective-permute-done.5) | copy-start | bytes 122884
  86.8 17.0 %collective-permute-start.6 = (bf16[16,6,1,320]{3,2,1,0:T(2,128)(2,1)}, bf16[16,6,1,320]{3,2,1,0:T(2,128)(2,1)S(1)}, u32[]{:S(2)}, u32[]{:S(2)}) collective-permute-start(bf16[16,6,1,320]{3,2,1,0:T(2,128)(2,1)} %get-tuple-element.114), channel_id=1, source_target_pairs={{0,1},{1,2},{2,3},{3,4},{4,5},{5,6},{6,7},{7,8},{8,9},{9,10},{10,1... | collective-permute-start | bytes 184328 | tf_op jit(solution)/shard_map/ppermute | solution.py:15
  88.7 15.7 %collective-permute-start.7 = (bf16[16,6,1,320]{3,2,1,0:T(2,128)(2,1)}, bf16[16,6,1,320]{3,2,1,0:T(2,128)(2,1)}, u32[]{:S(2)}, u32[]{:S(2)}) collective-permute-start(bf16[16,6,1,320]{3,2,1,0:T(2,128)(2,1)} %get-tuple-element.115), channel_id=1, source_target_pairs={{1,0},{2,1},{3,2},{4,3},{5,4},{6,5},{7,6},{8,7},{9,8},{10,9},{11,1... | collective-permute-start | bytes 184328 | tf_op jit(solution)/shard_map/ppermute | solution.py:16
  103.8 0.7 copy-start.18
  109.7 7.2 %copy-start.7 = (bf16[256,320]{1,0:T(8,128)(2,1)S(1)}, bf16[256,320]{1,0:T(8,128)(2,1)}, u32[]{:S(2)}) copy-start(bf16[256,320]{1,0:T(8,128)(2,1)} %reshape.173) | copy-start | bytes 491524
  116.6 1.9 copy-start.10
  116.6 2.2 copy-start.3
  117.0 2.2 copy-start.8
  117.3 2.3 copy-start.9
  118.6 1.3 copy-start.5
  120.6 27.4 %copy-start.2 = (bf16[16,4,4,320]{3,2,1,0:T(4,128)(2,1)}, bf16[16,4,4,320]{3,2,1,0:T(4,128)(2,1)S(1)}, u32[]{:S(2)}) copy-start(bf16[16,4,4,320]{3,2,1,0:T(4,128)(2,1)S(1)} %fusion.36) | copy-start | bytes 491524
  145.4 14.5 %copy-start.19 = (bf16[3,64,320]{2,1,0:T(8,128)(2,1)S(1)}, bf16[3,64,320]{2,1,0:T(8,128)(2,1)}, u32[]{:S(2)}) copy-start(bf16[3,64,320]{2,1,0:T(8,128)(2,1)} %param.11) | copy-start | bytes 368644
  145.4 17.6 %copy-start.21 = (bf16[2,64]{1,0:T(2,128)(2,1)S(1)}, bf16[2,64]{1,0:T(2,128)(2,1)}, u32[]{:S(2)}) copy-start(bf16[2,64]{1,0:T(2,128)(2,1)} %param.12) | copy-start | bytes 772
  145.4 19.8 %copy-start.20 = (bf16[64,320]{1,0:T(8,128)(2,1)S(1)}, bf16[64,320]{1,0:T(8,128)(2,1)}, u32[]{:S(2)}) copy-start(bf16[64,320]{1,0:T(8,128)(2,1)} %param.13) | copy-start | bytes 122884
  148.0 83.3 %all-to-all-start.1 = ((bf16[32,32,2,320]{3,2,1,0:T(2,128)(2,1)}), bf16[32,32,2,320]{3,2,1,0:T(2,128)(2,1)S(1)}, u32[]{:S(2)}, u32[]{:S(2)}) async-start(bf16[32,32,2,320]{3,2,1,0:T(2,128)(2,1)} %stack.3), calls=%async_computation.1 | async-start | bytes 3145728 | tf_op jit(solution)/shard_map/all_to_all | solution.py:77
  159.8 34.8 %collective-permute-start.8 = (bf16[3,64,320]{2,1,0:T(8,128)(2,1)S(1)}, bf16[3,64,320]{2,1,0:T(8,128)(2,1)S(1)}, u32[]{:S(2)}, u32[]{:S(2)}) collective-permute-start(bf16[3,64,320]{2,1,0:T(8,128)(2,1)S(1)} %copy-done.19), channel_id=1, source_target_pairs={{0,1},{1,0},{2,3},{3,2},{4,5},{5,4},{6,7},{7,6},{8,9},{9,8},{10,11... | collective-permute-start | bytes 368648 | tf_op jit(solution)/shard_map/ppermute | solution.py:22
  163.0 29.2 %collective-permute-start.9 = (bf16[2,64]{1,0:T(2,128)(2,1)S(1)}, bf16[2,64]{1,0:T(2,128)(2,1)S(1)}, u32[]{:S(2)}, u32[]{:S(2)}) collective-permute-start(bf16[2,64]{1,0:T(2,128)(2,1)S(1)} %copy-done.21), channel_id=1, source_target_pairs={{0,1},{1,0},{2,3},{3,2},{4,5},{5,4},{6,7},{7,6},{8,9},{9,8},{10,11... | collective-permute-start | bytes 776 | tf_op jit(solution)/shard_map/ppermute | solution.py:22
  165.3 28.7 %collective-permute-start.10 = (bf16[64,320]{0,1:T(8,128)(2,1)S(1)}, bf16[64,320]{0,1:T(8,128)(2,1)S(1)}, u32[]{:S(2)}, u32[]{:S(2)}) collective-permute-start(bf16[64,320]{0,1:T(8,128)(2,1)S(1)} %copy.90), channel_id=1, source_target_pairs={{0,1},{1,0},{2,3},{3,2},{4,5},{5,4},{6,7},{7,6},{8,9},{9,8},{10,11... | collective-permute-start | bytes 122888 | tf_op jit(solution)/shard_map/ppermute | solution.py:22
  242.2 1.6 copy-start.12
  242.2 1.6 copy-start.17
  243.9 5.1 %copy-start.15 = (bf16[64,320]{0,1:T(8,128)(2,1)S(1)}, bf16[64,320]{0,1:T(8,128)(2,1)}, u32[]{:S(2)}) copy-start(bf16[64,320]{0,1:T(8,128)(2,1)} %get-tuple-element.128) | copy-start | bytes 122884
  243.9 5.1 %copy-start.16 = (bf16[64,320]{0,1:T(8,128)(2,1)S(1)}, bf16[64,320]{0,1:T(8,128)(2,1)}, u32[]{:S(2)}) copy-start(bf16[64,320]{0,1:T(8,128)(2,1)} %get-tuple-element.129) | copy-start | bytes 122884
  250.6 48.9 %all-to-all-start.2 = ((bf16[32,32,1,320]{3,0,2,1:T(8,128)(2,1)}), bf16[32,32,1,320]{3,0,2,1:T(8,128)(2,1)S(1)}, u32[]{:S(2)}, u32[]{:S(2)}) async-start(bf16[32,32,1,320]{3,0,2,1:T(8,128)(2,1)} %copy.92), calls=%async_computation.2 | async-start | bytes 1572864 | tf_op jit(solution)/shard_map/all_to_all | solution.py:113
